TPU v7x, 32 devices: a whole 2x2x4 slice. The times are simulated.
32 devices in a mesh: row: 4 (over x, core), col: 8 (over z, y).
Axes of the slice: x: 2, y: 2, z: 4, core: 2. Of those that a mesh axis runs over, the one named last changes fastest.
Arguments:
- vectors: float32 [8, 4096], P(None, ('row', 'col')), may hold values from -6 to 6
- diagonal: float32 [4096], P(('row', 'col'))
- blocks: float32 [4, 8, 8, 128, 128], P('row', 'col'), may hold values from -0.125 to 0.125
- block_rows: int32 [4, 8, 8], P('row', 'col'), may hold values from 0 to 7
- block_cols: int32 [4, 8, 8], P('row', 'col'), may hold values from 0 to 3
- counts: int32 [4, 8], P('row', 'col'), may hold values from 4 to 8, as said below
Outputs:
- eigvecs: float32 [8, 4096], P(None, ('row', 'col'))
- factor: float32 [8, 8], replicated
Inputs may be any that keep to these rules, and one draw needn't show every extreme that they name: `counts`: every device has at least half of its 8 slots live, and some device has all 8 live.
All inputs are finite; a program needn't handle non-finite values.
Results may differ from a plain program's by a relative error of at most 0.0001.
Values sent between devices are 32-bit elements; how exact they have to be, the bound alone decides.
No kernel may reach another device: no remote copies, remote signals or barrier semaphores. Data moves between devices by JAX's collectives and lax.ppermute only.
A program may use at most 64 MiB of HBM per device.

v0:
```python
import jax
import jax.numpy as jnp
from jax import lax
from jax.sharding import PartitionSpec as P

ITERS = 4


def solve_lower(lower, values):
    return lax.linalg.triangular_solve(lower, values, left_side=True, lower=True)


def apply_tile(tile, rows_local, cols_local, live, current, col_vectors, row_vectors):
    high = lax.Precision.HIGHEST
    nvec = current.shape[0]
    width = tile.shape[-1]
    col_count = col_vectors.shape[1] // width
    row_count = row_vectors.shape[1] // width
    slots = jnp.arange(rows_local.shape[0])
    mask = (slots < live).astype(jnp.float32)
    row_select = (rows_local[:, None] == jnp.arange(row_count)[None, :]).astype(jnp.float32) * mask[
        :, None
    ]
    col_select = (cols_local[:, None] == jnp.arange(col_count)[None, :]).astype(jnp.float32) * mask[
        :, None
    ]
    col_input = jnp.einsum(
        "bq,kqj->kbj", col_select, col_vectors.reshape(nvec, col_count, width), precision=high
    )
    direct = jnp.einsum("bij,kbj->kbi", tile, col_input, precision=high)
    direct_part = jnp.einsum("bq,kbi->kqi", row_select, direct, precision=high).reshape(
        nvec, row_count * width
    )
    row_input = jnp.einsum(
        "bq,kqi->kbi", row_select, row_vectors.reshape(nvec, row_count, width), precision=high
    )
    transposed = jnp.einsum("bij,kbi->kbj", tile, row_input, precision=high)
    transposed_part = jnp.einsum("bq,kbj->kqj", col_select, transposed, precision=high).reshape(
        nvec, col_count * width
    )
    direct_sum = lax.psum_scatter(direct_part, "col", scatter_dimension=1, tiled=True)
    transposed_sum = lax.psum_scatter(transposed_part, "row", scatter_dimension=1, tiled=True)
    return (direct_sum, transposed_sum)


def gram_factor(images):
    local_gram = jnp.dot(
        images, images.T, precision=lax.Precision.HIGHEST, preferred_element_type=jnp.float32
    )
    gram = lax.psum(local_gram, ("row", "col"))
    return jnp.linalg.cholesky(gram)


def shards(vectors, diagonal, blocks, block_rows, block_cols, counts):
    tile = blocks[0, 0]
    rows_local = block_rows[0, 0]
    cols_local = block_cols[0, 0]
    live = counts[0, 0]
    nvec = vectors.shape[0]
    current = vectors
    lower = jnp.eye(nvec, dtype=jnp.float32)
    for step in range(ITERS):
        col_vectors = lax.all_gather(current, "row", axis=1, tiled=True)
        row_vectors = lax.all_gather(current, "col", axis=1, tiled=True)
        direct_sum, transposed_sum = apply_tile(
            tile, rows_local, cols_local, live, current, col_vectors, row_vectors
        )
        images = diagonal[None, :] * current + direct_sum + transposed_sum
        lower = gram_factor(images)
        current = solve_lower(lower, images)
    return (current, lower)


def solution(mesh):
    placed = (
        P(None, ("row", "col")),
        P(("row", "col")),
        P("row", "col", None, None, None),
        P("row", "col", None),
        P("row", "col", None),
        P("row", "col"),
    )
    return jax.shard_map(
        shards,
        mesh=mesh,
        in_specs=placed,
        out_specs=(P(None, ("row", "col")), P()),
        check_vma=False,
    )
```

profile of v0, /device:TPU:0, one launch (start us, length us, event | category | flops | bytes accessed | tf_op | source)
XLA Modules:
  0.0 656.2 jit_solution(13595704017735790086)
XLA Ops:
  7.9 32.4 %all_gather.25 = f32[8,1024]{1,0:T(8,128)S(1)} all-gather(f32[8,128]{1,0:T(8,128)S(1)} %copy-done.1), channel_id=1, replica_groups=mesh['row'=4,'col'=8] {'col'}, dimensions={1}, use_global_device_ids=true | all-gather | bytes 36864 | tf_op jit(solution)/shard_map/all_gather | solution.py:64
  40.4 0.7 copy-done.3
  41.8 0.7 copy-done.2
  43.3 5.2 all_gather.24
  48.7 0.9 fusion.14
  50.5 13.4 %reduce-scatter.11.cloned.1.call-done = f32[8,128]{1,0:T(8,128)} async-done(((f32[8,512]{1,0:T(8,128)}), f32[8,128]{1,0:T(8,128)}) %reduce-scatter.11.cloned.1.call-update) | async-done | bytes 4112 | tf_op jit(solution)/shard_map/reduce_scatter | solution.py:42
  63.9 57.9 %reduce-scatter.9.cloned.1.call-done = f32[8,128]{1,0:T(8,128)} async-done(((f32[8,1024]{1,0:T(8,128)}), f32[8,128]{1,0:T(8,128)}) %reduce-scatter.9.cloned.1.call-update) | async-done | bytes 4112 | tf_op jit(solution)/shard_map/reduce_scatter | solution.py:41
  121.8 0.7 add_add_fusion.3
  122.6 40.1 %psum.28 = f32[8,8]{0,1:T(8,128)S(1)} all-reduce(f32[8,8]{0,1:T(8,128)S(1)} %fusion.165), channel_id=1, replica_groups=mesh['row'=4,'col'=8] {'row','col'}, use_global_device_ids=true, to_apply=%region_2.0 | all-reduce | flops 64 | bytes 512 | tf_op jit(solution)/shard_map/psum | solution.py:50
  162.8 0.7 cholesky.74
  163.5 0.6 compare_reduce_fusion.3
  164.2 0.6 fusion.46
  165.7 5.5 all_gather.26
  171.2 30.6 %all_gather.27 = f32[8,1024]{1,0:T(8,128)S(1)} all-gather(f32[8,128]{1,0:T(8,128)S(1)} %fusion.55), channel_id=1, replica_groups=mesh['row'=4,'col'=8] {'col'}, dimensions={1}, use_global_device_ids=true | all-gather | bytes 36864 | tf_op jit(solution)/shard_map/all_gather | solution.py:64
  201.8 1.0 convolution_bitcast_fusion.5
  203.0 0.9 fusion.10
  203.9 1.0 convolution_bitcast_fusion.2
  207.3 17.4 %reduce-scatter.15.cloned.1.call-done = f32[8,128]{1,0:T(8,128)} async-done(((f32[8,512]{1,0:T(8,128)}), f32[8,128]{1,0:T(8,128)}) %reduce-scatter.15.cloned.1.call-update) | async-done | bytes 4112 | tf_op jit(solution)/shard_map/reduce_scatter | solution.py:42
  224.7 57.8 %reduce-scatter.13.cloned.1.call-done = f32[8,128]{1,0:T(8,128)} async-done(((f32[8,1024]{1,0:T(8,128)}), f32[8,128]{1,0:T(8,128)}) %reduce-scatter.13.cloned.1.call-update) | async-done | bytes 4112 | tf_op jit(solution)/shard_map/reduce_scatter | solution.py:41
  282.5 0.7 add_add_fusion.2
  283.3 40.1 %psum.29 = f32[8,8]{0,1:T(8,128)S(1)} all-reduce(f32[8,8]{0,1:T(8,128)S(1)} %fusion.166), channel_id=1, replica_groups=mesh['row'=4,'col'=8] {'row','col'}, use_global_device_ids=true, to_apply=%region_7.10 | all-reduce | flops 64 | bytes 512 | tf_op jit(solution)/shard_map/psum | solution.py:50
  323.5 0.7 cholesky.85
  324.2 0.6 compare_reduce_fusion.2
  324.9 0.6 fusion.47
  326.4 5.5 all_gather.28
  331.9 30.6 %all_gather.29 = f32[8,1024]{1,0:T(8,128)S(1)} all-gather(f32[8,128]{1,0:T(8,128)S(1)} %fusion.53), channel_id=1, replica_groups=mesh['row'=4,'col'=8] {'col'}, dimensions={1}, use_global_device_ids=true | all-gather | bytes 36864 | tf_op jit(solution)/shard_map/all_gather | solution.py:64
  362.5 1.0 convolution_bitcast_fusion.4
  363.7 0.9 fusion.6
  364.6 1.0 convolution_bitcast_fusion.1
  368.0 17.4 %reduce-scatter.19.cloned.1.call-done = f32[8,128]{1,0:T(8,128)} async-done(((f32[8,512]{1,0:T(8,128)}), f32[8,128]{1,0:T(8,128)}) %reduce-scatter.19.cloned.1.call-update) | async-done | bytes 4112 | tf_op jit(solution)/shard_map/reduce_scatter | solution.py:42
  385.4 57.8 %reduce-scatter.17.cloned.1.call-done = f32[8,128]{1,0:T(8,128)} async-done(((f32[8,1024]{1,0:T(8,128)}), f32[8,128]{1,0:T(8,128)}) %reduce-scatter.17.cloned.1.call-update) | async-done | bytes 4112 | tf_op jit(solution)/shard_map/reduce_scatter | solution.py:41
  443.2 0.7 add_add_fusion.1
  444.1 40.3 %psum.30 = f32[8,8]{0,1:T(8,128)S(1)} all-reduce(f32[8,8]{0,1:T(8,128)S(1)} %fusion.167), channel_id=1, replica_groups=mesh['row'=4,'col'=8] {'row','col'}, use_global_device_ids=true, to_apply=%region_10.13 | all-reduce | flops 64 | bytes 512 | tf_op jit(solution)/shard_map/psum | solution.py:50
  484.4 0.7 cholesky.96
  485.1 0.6 compare_reduce_fusion.1
  485.8 0.6 fusion.48
  487.3 5.5 all_gather.30
  492.8 30.6 %all_gather.31 = f32[8,1024]{1,0:T(8,128)S(1)} all-gather(f32[8,128]{1,0:T(8,128)S(1)} %fusion.51), channel_id=1, replica_groups=mesh['row'=4,'col'=8] {'col'}, dimensions={1}, use_global_device_ids=true | all-gather | bytes 36864 | tf_op jit(solution)/shard_map/all_gather | solution.py:64
  523.4 1.0 convolution_bitcast_fusion.3
  524.6 0.9 fusion.2
  525.5 1.0 convolution_bitcast_fusion
  528.9 17.5 %reduce-scatter.23.cloned.1.call-done = f32[8,128]{1,0:T(8,128)} async-done(((f32[8,512]{1,0:T(8,128)}), f32[8,128]{1,0:T(8,128)}) %reduce-scatter.23.cloned.1.call-update) | async-done | bytes 4112 | tf_op jit(solution)/shard_map/reduce_scatter | solution.py:42
  546.4 57.9 %reduce-scatter.21.cloned.1.call-done = f32[8,128]{1,0:T(8,128)} async-done(((f32[8,1024]{1,0:T(8,128)}), f32[8,128]{1,0:T(8,128)}) %reduce-scatter.21.cloned.1.call-update) | async-done | bytes 4112 | tf_op jit(solution)/shard_map/reduce_scatter | solution.py:41
  604.3 0.7 add_add_fusion
  605.1 40.1 %psum.31 = f32[8,8]{0,1:T(8,128)S(1)} all-reduce(f32[8,8]{0,1:T(8,128)S(1)} %fusion.168), channel_id=1, replica_groups=mesh['row'=4,'col'=8] {'row','col'}, use_global_device_ids=true, to_apply=%region_13.16 | all-reduce | flops 64 | bytes 512 | tf_op jit(solution)/shard_map/psum | solution.py:50
  645.3 0.7 cholesky.107
  646.7 1.2 select_bitcast_fusion
  648.6 0.8 fusion.49
  (77 shorter events, 15.0 us)
Async XLA Ops:
  7.2 34.1 %copy-start = (f32[1,1,8,128,128]{4,3,2,1,0:T(8,128)S(1)}, f32[1,1,8,128,128]{4,3,2,1,0:T(8,128)}, u32[]{:S(2)}) copy-start(f32[1,1,8,128,128]{4,3,2,1,0:T(8,128)} %param.11) | copy-start | bytes 1572868
  7.2 0.8 copy-start.1
  7.2 56.7 %reduce-scatter.11.cloned.1.call-start = ((), (), s32[]{:S(2)}) async-start(), calls=%async_computation.9 | async-start | bytes 20480 | tf_op jit(solution)/shard_map/reduce_scatter | solution.py:42
  40.4 0.7 copy-start.3
  41.8 0.7 copy-start.2
  43.2 78.5 %reduce-scatter.9.cloned.1.call-start = ((), (), s32[]{:S(2)}) async-start(), calls=%async_computation.8 | async-start | bytes 36864 | tf_op jit(solution)/shard_map/reduce_scatter | solution.py:41
  50.5 71.3 %copy-start.4 = (f32[128]{0:T(128)S(1)}, f32[128]{0:T(128)}, u32[]{:S(2)}) copy-start(f32[128]{0:T(128)} %param.10) | copy-start | bytes 1540
  50.5 174.3 %reduce-scatter.15.cloned.1.call-start = ((), (), s32[]{:S(2)}) async-start(), calls=%async_computation.11 | async-start | bytes 20480 | tf_op jit(solution)/shard_map/reduce_scatter | solution.py:42
  206.4 76.0 %reduce-scatter.13.cloned.1.call-start = ((), (), s32[]{:S(2)}) async-start(), calls=%async_computation.10 | async-start | bytes 36864 | tf_op jit(solution)/shard_map/reduce_scatter | solution.py:41
  207.3 178.1 %reduce-scatter.19.cloned.1.call-start = ((), (), s32[]{:S(2)}) async-start(), calls=%async_computation.13 | async-start | bytes 20480 | tf_op jit(solution)/shard_map/reduce_scatter | solution.py:42
  367.1 76.1 %reduce-scatter.17.cloned.1.call-start = ((), (), s32[]{:S(2)}) async-start(), calls=%async_computation.12 | async-start | bytes 36864 | tf_op jit(solution)/shard_map/reduce_scatter | solution.py:41
  368.0 178.4 %reduce-scatter.23.cloned.1.call-start = ((), (), s32[]{:S(2)}) async-start(), calls=%async_computation.15 | async-start | bytes 20480 | tf_op jit(solution)/shard_map/reduce_scatter | solution.py:42
  528.0 76.2 %reduce-scatter.21.cloned.1.call-start = ((), (), s32[]{:S(2)}) async-start(), calls=%async_computation.14 | async-start | bytes 36864 | tf_op jit(solution)/shard_map/reduce_scatter | solution.py:41
Sparse Core Ops, SparseCore 0:
  43.4 20.4 reduce-scatter.10
  67.0 54.6 reduce-scatter.8
  206.6 18.1 reduce-scatter.14
  227.7 54.7 reduce-scatter.12
  367.3 18.1 reduce-scatter.18
  388.4 54.7 reduce-scatter.16
  528.2 18.1 reduce-scatter.22
  549.5 54.7 reduce-scatter.20
where the time goes:
time: 657 us; the launch traced here: 656 us
  blocking collectives  307 us (47%)
  waiting for transfers between devices  297 us (45%)
  matrix products  15.5 us (2%)
  between operations  15 us (2%)
  other arithmetic  14 us (2%)
  local copies, waits for them, and re-layouts  7.5 us (1%)
    reduce_scatter x4, waiting for transfers between devices, apply_tile(): lax.psum_scatter(direct_part, 'col', scatter_dimension=1, tiled=True)  231 us
    psum x4, blocking collectives, gram_factor(): gram = lax.psum(local_gram, ('row', 'col'))  161 us
    all_gather x4, blocking collectives, shards(): row_vectors = lax.all_gather(current, 'col', axis=1, tiled=True)  124 us
    reduce_scatter x4, waiting for transfers between devices, apply_tile(): lax.psum_scatter(transposed_part, 'row', scatter_dimension=1, tiled=True)  65.6 us
    all_gather x4, blocking collectives, shards(): col_vectors = lax.all_gather(current, 'row', axis=1, tiled=True)  21.9 us
  transfers between devices with their start and end apart: 8, of which 8 were waited for; matrix products, arithmetic and copies ran while one was open for 1% of the time, Pallas kernels for 0%

commit v1 on v0

--- a/solution.py
+++ b/solution.py
@@ -61,7 +61,25 @@
     lower = jnp.eye(nvec, dtype=jnp.float32)
     for step in range(ITERS):
         col_vectors = lax.all_gather(current, "row", axis=1, tiled=True)
-        row_vectors = lax.all_gather(current, "col", axis=1, tiled=True)
+        ways, here, lap = (lax.axis_size("col"), lax.axis_index("col"), current.shape[1])
+        lengths = [n * ways if d == 1 else n for d, n in enumerate(current.shape)]
+        full = lax.dynamic_update_slice_in_dim(
+            jnp.zeros(lengths, current.dtype), current, here * lap, axis=1
+        )
+        going_up = going_down = current
+        for far in range(1, ways // 2 + 1):
+            going_up = lax.ppermute(going_up, "col", [(d, (d + 1) % ways) for d in range(ways)])
+            full = lax.dynamic_update_slice_in_dim(
+                full, going_up, (here - far) % ways * lap, axis=1
+            )
+            if 2 * far < ways:
+                going_down = lax.ppermute(
+                    going_down, "col", [(d, (d - 1) % ways) for d in range(ways)]
+                )
+                full = lax.dynamic_update_slice_in_dim(
+                    full, going_down, (here + far) % ways * lap, axis=1
+                )
+        row_vectors = full
         direct_sum, transposed_sum = apply_tile(
             tile, rows_local, cols_local, live, current, col_vectors, row_vectors
         )

time: 657 us -> 631 us (0.960)
  blocking collectives: 307 us -> 182 us
  starting transfers between devices: 0.33 us -> 58.5 us
  waiting for transfers between devices: 297 us -> 335 us
    all_gather x4 -> x0, blocking collectives: 124 us -> none  [shards(): row_vectors = lax.all_gather(current, 'col', axis=1, tiled=True)]
    ppermute x0 -> x28, starting transfers between devices: none -> 58.1 us  [the longest x12 48.1 us: shards(): lax.ppermute(going_down, 'col', [(d, (d - 1) % ways) for d in range(ways)])]
    ppermute x0 -> x28, waiting for transfers between devices: none -> 37.7 us  [the longest x16 37.7 us: shards(): lax.ppermute(going_up, 'col', [(d, (d + 1) % ways) for d in range(ways)])]
  transfers between devices with their start and end apart: 8 -> 36, of which waited for: 8 -> 20; matrix products, arithmetic and copies ran while one was open for 1% -> 2% of each run, Pallas kernels for 0% -> 0%
where the time goes in v1:
time: 631 us; the launch traced here: 630 us
  waiting for transfers between devices  335 us (53%)
  blocking collectives  182 us (29%)
  starting transfers between devices  58.5 us (9%)
  matrix products  16.3 us (3%)
  between operations  15.2 us (2%)
  other arithmetic  14.1 us (2%)
  local copies, waits for them, and re-layouts  8.46 us (1%)
    reduce_scatter x4, waiting for transfers between devices, apply_tile(): lax.psum_scatter(direct_part, 'col', scatter_dimension=1, tiled=True)  231 us
    psum x4, blocking collectives, gram_factor(): gram = lax.psum(local_gram, ('row', 'col'))  160 us
    reduce_scatter x4, waiting for transfers between devices, apply_tile(): lax.psum_scatter(transposed_part, 'row', scatter_dimension=1, tiled=True)  65.6 us
    ppermute x12, starting transfers between devices, shards(): lax.ppermute(going_down, 'col', [(d, (d - 1) % ways) for d in range(ways)])  48.1 us
    ppermute x16, waiting for transfers between devices, shards(): lax.ppermute(going_up, 'col', [(d, (d + 1) % ways) for d in range(ways)])  37.7 us
    all_gather x4, blocking collectives, shards(): col_vectors = lax.all_gather(current, 'row', axis=1, tiled=True)  22 us
  transfers between devices with their start and end apart: 36, of which 20 were waited for; matrix products, arithmetic and copies ran while one was open for 2% of the time, Pallas kernels for 0%

profile of v1, /device:TPU:0, one launch (start us, length us, event | category | flops | bytes accessed | tf_op | source)
XLA Modules:
  0.0 629.7 jit_solution(4906009306303666219)
XLA Ops:
  7.2 3.0 collective-permute-start
  10.3 3.1 collective-permute-start.1
  14.1 5.2 all_gather.12
  21.9 4.7 collective-permute-start.3
  26.6 1.6 collective-permute-done.2
  28.2 4.7 collective-permute-start.5
  32.9 1.6 collective-permute-done.4
  34.5 6.3 collective-permute-done.6
  44.9 16.1 %reduce-scatter.11.cloned.1.call-done = f32[8,128]{1,0:T(8,128)} async-done(((f32[8,512]{1,0:T(8,128)}), f32[8,128]{1,0:T(8,128)}) %reduce-scatter.11.cloned.1.call-update) | async-done | bytes 4112 | tf_op jit(solution)/shard_map/reduce_scatter | solution.py:42
  61.0 57.9 %reduce-scatter.9.cloned.1.call-done = f32[8,128]{1,0:T(8,128)} async-done(((f32[8,1024]{1,0:T(8,128)}), f32[8,128]{1,0:T(8,128)}) %reduce-scatter.9.cloned.1.call-update) | async-done | bytes 4112 | tf_op jit(solution)/shard_map/reduce_scatter | solution.py:41
  119.7 40.1 %psum.28 = f32[8,8]{0,1:T(8,128)S(1)} all-reduce(f32[8,8]{0,1:T(8,128)S(1)} %fusion.162), channel_id=1, replica_groups=mesh['row'=4,'col'=8] {'row','col'}, use_global_device_ids=true, to_apply=%region_2.3 | all-reduce | flops 64 | bytes 512 | tf_op jit(solution)/shard_map/psum | solution.py:50
  162.8 2.3 collective-permute-start.7
  165.1 2.5 collective-permute-start.8
  167.5 5.5 all_gather.13
  175.2 4.7 collective-permute-start.10
  179.9 1.6 collective-permute-done.9
  181.5 4.7 collective-permute-start.12
  186.2 1.6 collective-permute-done.11
  187.8 6.3 collective-permute-done.13
  194.1 1.0 convolution_bitcast_fusion.2
  197.5 16.5 %reduce-scatter.15.cloned.1.call-done = f32[8,128]{1,0:T(8,128)} async-done(((f32[8,512]{1,0:T(8,128)}), f32[8,128]{1,0:T(8,128)}) %reduce-scatter.15.cloned.1.call-update) | async-done | bytes 4112 | tf_op jit(solution)/shard_map/reduce_scatter | solution.py:42
  214.0 57.8 %reduce-scatter.13.cloned.1.call-done = f32[8,128]{1,0:T(8,128)} async-done(((f32[8,1024]{1,0:T(8,128)}), f32[8,128]{1,0:T(8,128)}) %reduce-scatter.13.cloned.1.call-update) | async-done | bytes 4112 | tf_op jit(solution)/shard_map/reduce_scatter | solution.py:41
  272.6 40.1 %psum.29 = f32[8,8]{0,1:T(8,128)S(1)} all-reduce(f32[8,8]{0,1:T(8,128)S(1)} %fusion.163), channel_id=1, replica_groups=mesh['row'=4,'col'=8] {'row','col'}, use_global_device_ids=true, to_apply=%region_7.10 | all-reduce | flops 64 | bytes 512 | tf_op jit(solution)/shard_map/psum | solution.py:50
  315.6 2.3 collective-permute-start.14
  317.9 2.5 collective-permute-start.15
  320.3 5.7 all_gather.14
  328.2 4.7 collective-permute-start.17
  332.9 1.6 collective-permute-done.16
  334.5 4.7 collective-permute-start.19
  339.2 1.6 collective-permute-done.18
  340.8 6.3 collective-permute-done.20
  347.1 1.0 convolution_bitcast_fusion.1
  350.5 16.5 %reduce-scatter.19.cloned.1.call-done = f32[8,128]{1,0:T(8,128)} async-done(((f32[8,512]{1,0:T(8,128)}), f32[8,128]{1,0:T(8,128)}) %reduce-scatter.19.cloned.1.call-update) | async-done | bytes 4112 | tf_op jit(solution)/shard_map/reduce_scatter | solution.py:42
  367.0 57.8 %reduce-scatter.17.cloned.1.call-done = f32[8,128]{1,0:T(8,128)} async-done(((f32[8,1024]{1,0:T(8,128)}), f32[8,128]{1,0:T(8,128)}) %reduce-scatter.17.cloned.1.call-update) | async-done | bytes 4112 | tf_op jit(solution)/shard_map/reduce_scatter | solution.py:41
  425.6 40.1 %psum.30 = f32[8,8]{0,1:T(8,128)S(1)} all-reduce(f32[8,8]{0,1:T(8,128)S(1)} %fusion.164), channel_id=1, replica_groups=mesh['row'=4,'col'=8] {'row','col'}, use_global_device_ids=true, to_apply=%region_10.13 | all-reduce | flops 64 | bytes 512 | tf_op jit(solution)/shard_map/psum | solution.py:50
  468.6 2.3 collective-permute-start.21
  470.9 2.5 collective-permute-start.22
  473.4 5.5 all_gather.15
  481.1 4.7 collective-permute-start.24
  485.8 1.6 collective-permute-done.23
  487.3 4.7 collective-permute-start.26
  492.1 1.6 collective-permute-done.25
  493.7 6.3 collective-permute-done.27
  499.9 1.0 convolution_bitcast_fusion
  503.3 16.5 %reduce-scatter.23.cloned.1.call-done = f32[8,128]{1,0:T(8,128)} async-done(((f32[8,512]{1,0:T(8,128)}), f32[8,128]{1,0:T(8,128)}) %reduce-scatter.23.cloned.1.call-update) | async-done | bytes 4112 | tf_op jit(solution)/shard_map/reduce_scatter | solution.py:42
  519.8 58.0 %reduce-scatter.21.cloned.1.call-done = f32[8,128]{1,0:T(8,128)} async-done(((f32[8,1024]{1,0:T(8,128)}), f32[8,128]{1,0:T(8,128)}) %reduce-scatter.21.cloned.1.call-update) | async-done | bytes 4112 | tf_op jit(solution)/shard_map/reduce_scatter | solution.py:41
  578.6 40.1 %psum.31 = f32[8,8]{0,1:T(8,128)S(1)} all-reduce(f32[8,8]{0,1:T(8,128)S(1)} %fusion.165), channel_id=1, replica_groups=mesh['row'=4,'col'=8] {'row','col'}, use_global_device_ids=true, to_apply=%region_13.16 | all-reduce | flops 64 | bytes 512 | tf_op jit(solution)/shard_map/psum | solution.py:50
  620.2 1.2 select_bitcast_fusion
  (163 shorter events, 35.2 us)
Async XLA Ops:
  7.2 13.7 %copy-start = (f32[1,1,8,128,128]{4,3,2,1,0:T(8,128)S(1)}, f32[1,1,8,128,128]{4,3,2,1,0:T(8,128)}, u32[]{:S(2)}) copy-start(f32[1,1,8,128,128]{4,3,2,1,0:T(8,128)} %param.11) | copy-start | bytes 1572868
  7.2 53.8 %reduce-scatter.11.cloned.1.call-start = ((), (), s32[]{:S(2)}) async-start(), calls=%async_computation.9 | async-start | bytes 20480 | tf_op jit(solution)/shard_map/reduce_scatter | solution.py:42
  7.2 14.6 %collective-permute-start = (f32[8,128]{1,0:T(8,128)}, f32[8,128]{1,0:T(8,128)S(1)}, u32[]{:S(2)}, u32[]{:S(2)}) collective-permute-start(f32[8,128]{1,0:T(8,128)} %param.9), channel_id=1, source_target_pairs={{0,1},{1,2},{2,3},{3,4},{4,5},{5,6},{6,7},{7,0},{8,9},{9,10},{10,1... | collective-permute-start | bytes 12296 | tf_op jit(solution)/shard_map/ppermute | solution.py:71
  10.3 11.6 %collective-permute-start.1 = (f32[8,128]{1,0:T(8,128)}, f32[8,128]{1,0:T(8,128)S(1)}, u32[]{:S(2)}, u32[]{:S(2)}) collective-permute-start(f32[8,128]{1,0:T(8,128)} %param.9), channel_id=1, source_target_pairs={{0,7},{1,0},{2,1},{3,2},{4,3},{5,4},{6,5},{7,6},{8,15},{9,8},{10,9... | collective-permute-start | bytes 12296 | tf_op jit(solution)/shard_map/ppermute | solution.py:76
  13.4 0.7 copy-start.1
  20.0 0.7 copy-start.2
  21.8 6.4 %collective-permute-start.2 = (f32[8,128]{1,0:T(8,128)S(1)}, f32[8,128]{1,0:T(8,128)S(1)}, u32[]{:S(2)}, u32[]{:S(2)}) collective-permute-start(f32[8,128]{1,0:T(8,128)S(1)} %collective-permute-done), channel_id=1, source_target_pairs={{0,1},{1,2},{2,3},{3,4},{4,5},{5,6},{6,7},{7,0},{8,9},{9,10},{10,1... | collective-permute-start | bytes 12296 | tf_op jit(solution)/shard_map/ppermute | solution.py:71
  21.9 6.3 collective-permute-start.3
  28.2 6.3 %collective-permute-start.4 = (f32[8,128]{1,0:T(8,128)S(1)}, f32[8,128]{1,0:T(8,128)S(1)}, u32[]{:S(2)}, u32[]{:S(2)}) collective-permute-start(f32[8,128]{1,0:T(8,128)S(1)} %collective-permute-done.2), channel_id=1, source_target_pairs={{0,1},{1,2},{2,3},{3,4},{4,5},{5,6},{6,7},{7,0},{8,9},{9,10},{10,1... | collective-permute-start | bytes 12296 | tf_op jit(solution)/shard_map/ppermute | solution.py:71
  28.2 6.3 %collective-permute-start.5 = (f32[8,128]{1,0:T(8,128)S(1)}, f32[8,128]{1,0:T(8,128)S(1)}, u32[]{:S(2)}, u32[]{:S(2)}) collective-permute-start(f32[8,128]{1,0:T(8,128)S(1)} %collective-permute-done.3), channel_id=1, source_target_pairs={{0,7},{1,0},{2,1},{3,2},{4,3},{5,4},{6,5},{7,6},{8,15},{9,8},{10,9... | collective-permute-start | bytes 12296 | tf_op jit(solution)/shard_map/ppermute | solution.py:76
  34.5 6.3 %collective-permute-start.6 = (f32[8,128]{1,0:T(8,128)S(1)}, f32[8,128]{1,0:T(8,128)S(1)}, u32[]{:S(2)}, u32[]{:S(2)}) collective-permute-start(f32[8,128]{1,0:T(8,128)S(1)} %collective-permute-done.4), channel_id=1, source_target_pairs={{0,1},{1,2},{2,3},{3,4},{4,5},{5,6},{6,7},{7,0},{8,9},{9,10},{10,1... | collective-permute-start | bytes 12296 | tf_op jit(solution)/shard_map/ppermute | solution.py:71
  40.8 0.7 copy-start.3
  44.0 74.9 %reduce-scatter.9.cloned.1.call-start = ((), (), s32[]{:S(2)}) async-start(), calls=%async_computation.8 | async-start | bytes 36864 | tf_op jit(solution)/shard_map/reduce_scatter | solution.py:41
  44.8 74.1 %copy-start.4 = (f32[128]{0:T(128)S(1)}, f32[128]{0:T(128)}, u32[]{:S(2)}) copy-start(f32[128]{0:T(128)} %param.10) | copy-start | bytes 1540
  44.8 169.1 %reduce-scatter.15.cloned.1.call-start = ((), (), s32[]{:S(2)}) async-start(), calls=%async_computation.11 | async-start | bytes 20480 | tf_op jit(solution)/shard_map/reduce_scatter | solution.py:42
  162.8 12.4 %collective-permute-start.7 = (f32[8,128]{1,0:T(8,128)S(1)}, f32[8,128]{1,0:T(8,128)S(1)}, u32[]{:S(2)}, u32[]{:S(2)}) collective-permute-start(f32[8,128]{1,0:T(8,128)S(1)} %get-tuple-element.7), channel_id=1, source_target_pairs={{0,1},{1,2},{2,3},{3,4},{4,5},{5,6},{6,7},{7,0},{8,9},{9,10},{10,1... | collective-permute-start | bytes 12296 | tf_op jit(solution)/shard_map/ppermute | solution.py:71
  165.1 10.1 %collective-permute-start.8 = (f32[8,128]{1,0:T(8,128)S(1)}, f32[8,128]{1,0:T(8,128)S(1)}, u32[]{:S(2)}, u32[]{:S(2)}) collective-permute-start(f32[8,128]{1,0:T(8,128)S(1)} %get-tuple-element.7), channel_id=1, source_target_pairs={{0,7},{1,0},{2,1},{3,2},{4,3},{5,4},{6,5},{7,6},{8,15},{9,8},{10,9... | collective-permute-start | bytes 12296 | tf_op jit(solution)/shard_map/ppermute | solution.py:76
  175.1 6.3 %collective-permute-start.9 = (f32[8,128]{1,0:T(8,128)S(1)}, f32[8,128]{1,0:T(8,128)S(1)}, u32[]{:S(2)}, u32[]{:S(2)}) collective-permute-start(f32[8,128]{1,0:T(8,128)S(1)} %collective-permute-done.7), channel_id=1, source_target_pairs={{0,1},{1,2},{2,3},{3,4},{4,5},{5,6},{6,7},{7,0},{8,9},{9,10},{10,1... | collective-permute-start | bytes 12296 | tf_op jit(solution)/shard_map/ppermute | solution.py:71
  175.2 6.3 collective-permute-start.10
  181.5 6.3 %collective-permute-start.11 = (f32[8,128]{1,0:T(8,128)S(1)}, f32[8,128]{1,0:T(8,128)S(1)}, u32[]{:S(2)}, u32[]{:S(2)}) collective-permute-start(f32[8,128]{1,0:T(8,128)S(1)} %collective-permute-done.9), channel_id=1, source_target_pairs={{0,1},{1,2},{2,3},{3,4},{4,5},{5,6},{6,7},{7,0},{8,9},{9,10},{10,1... | collective-permute-start | bytes 12296 | tf_op jit(solution)/shard_map/ppermute | solution.py:71
  181.5 6.3 %collective-permute-start.12 = (f32[8,128]{1,0:T(8,128)S(1)}, f32[8,128]{1,0:T(8,128)S(1)}, u32[]{:S(2)}, u32[]{:S(2)}) collective-permute-start(f32[8,128]{1,0:T(8,128)S(1)} %collective-permute-done.10), channel_id=1, source_target_pairs={{0,7},{1,0},{2,1},{3,2},{4,3},{5,4},{6,5},{7,6},{8,15},{9,8},{10,9... | collective-permute-start | bytes 12296 | tf_op jit(solution)/shard_map/ppermute | solution.py:76
  187.8 6.3 %collective-permute-start.13 = (f32[8,128]{1,0:T(8,128)S(1)}, f32[8,128]{1,0:T(8,128)S(1)}, u32[]{:S(2)}, u32[]{:S(2)}) collective-permute-start(f32[8,128]{1,0:T(8,128)S(1)} %collective-permute-done.11), channel_id=1, source_target_pairs={{0,1},{1,2},{2,3},{3,4},{4,5},{5,6},{6,7},{7,0},{8,9},{9,10},{10,1... | collective-permute-start | bytes 12296 | tf_op jit(solution)/shard_map/ppermute | solution.py:71
  196.6 75.1 %reduce-scatter.13.cloned.1.call-start = ((), (), s32[]{:S(2)}) async-start(), calls=%async_computation.10 | async-start | bytes 36864 | tf_op jit(solution)/shard_map/reduce_scatter | solution.py:41
  197.5 169.5 %reduce-scatter.19.cloned.1.call-start = ((), (), s32[]{:S(2)}) async-start(), calls=%async_computation.13 | async-start | bytes 20480 | tf_op jit(solution)/shard_map/reduce_scatter | solution.py:42
  315.6 12.6 %collective-permute-start.14 = (f32[8,128]{1,0:T(8,128)S(1)}, f32[8,128]{1,0:T(8,128)S(1)}, u32[]{:S(2)}, u32[]{:S(2)}) collective-permute-start(f32[8,128]{1,0:T(8,128)S(1)} %get-tuple-element.9), channel_id=1, source_target_pairs={{0,1},{1,2},{2,3},{3,4},{4,5},{5,6},{6,7},{7,0},{8,9},{9,10},{10,1... | collective-permute-start | bytes 12296 | tf_op jit(solution)/shard_map/ppermute | solution.py:71
  317.9 10.3 %collective-permute-start.15 = (f32[8,128]{1,0:T(8,128)S(1)}, f32[8,128]{1,0:T(8,128)S(1)}, u32[]{:S(2)}, u32[]{:S(2)}) collective-permute-start(f32[8,128]{1,0:T(8,128)S(1)} %get-tuple-element.9), channel_id=1, source_target_pairs={{0,7},{1,0},{2,1},{3,2},{4,3},{5,4},{6,5},{7,6},{8,15},{9,8},{10,9... | collective-permute-start | bytes 12296 | tf_op jit(solution)/shard_map/ppermute | solution.py:76
  328.1 6.3 %collective-permute-start.16 = (f32[8,128]{1,0:T(8,128)S(1)}, f32[8,128]{1,0:T(8,128)S(1)}, u32[]{:S(2)}, u32[]{:S(2)}) collective-permute-start(f32[8,128]{1,0:T(8,128)S(1)} %collective-permute-done.14), channel_id=1, source_target_pairs={{0,1},{1,2},{2,3},{3,4},{4,5},{5,6},{6,7},{7,0},{8,9},{9,10},{10,1... | collective-permute-start | bytes 12296 | tf_op jit(solution)/shard_map/ppermute | solution.py:71
  328.2 6.3 collective-permute-start.17
  334.5 6.3 %collective-permute-start.18 = (f32[8,128]{1,0:T(8,128)S(1)}, f32[8,128]{1,0:T(8,128)S(1)}, u32[]{:S(2)}, u32[]{:S(2)}) collective-permute-start(f32[8,128]{1,0:T(8,128)S(1)} %collective-permute-done.16), channel_id=1, source_target_pairs={{0,1},{1,2},{2,3},{3,4},{4,5},{5,6},{6,7},{7,0},{8,9},{9,10},{10,1... | collective-permute-start | bytes 12296 | tf_op jit(solution)/shard_map/ppermute | solution.py:71
  334.5 6.3 %collective-permute-start.19 = (f32[8,128]{1,0:T(8,128)S(1)}, f32[8,128]{1,0:T(8,128)S(1)}, u32[]{:S(2)}, u32[]{:S(2)}) collective-permute-start(f32[8,128]{1,0:T(8,128)S(1)} %collective-permute-done.17), channel_id=1, source_target_pairs={{0,7},{1,0},{2,1},{3,2},{4,3},{5,4},{6,5},{7,6},{8,15},{9,8},{10,9... | collective-permute-start | bytes 12296 | tf_op jit(solution)/shard_map/ppermute | solution.py:76
  340.8 6.3 %collective-permute-start.20 = (f32[8,128]{1,0:T(8,128)S(1)}, f32[8,128]{1,0:T(8,128)S(1)}, u32[]{:S(2)}, u32[]{:S(2)}) collective-permute-start(f32[8,128]{1,0:T(8,128)S(1)} %collective-permute-done.18), channel_id=1, source_target_pairs={{0,1},{1,2},{2,3},{3,4},{4,5},{5,6},{6,7},{7,0},{8,9},{9,10},{10,1... | collective-permute-start | bytes 12296 | tf_op jit(solution)/shard_map/ppermute | solution.py:71
  349.6 75.2 %reduce-scatter.17.cloned.1.call-start = ((), (), s32[]{:S(2)}) async-start(), calls=%async_computation.12 | async-start | bytes 36864 | tf_op jit(solution)/shard_map/reduce_scatter | solution.py:41
  350.4 169.4 %reduce-scatter.23.cloned.1.call-start = ((), (), s32[]{:S(2)}) async-start(), calls=%async_computation.15 | async-start | bytes 20480 | tf_op jit(solution)/shard_map/reduce_scatter | solution.py:42
  468.6 12.4 %collective-permute-start.21 = (f32[8,128]{1,0:T(8,128)S(1)}, f32[8,128]{1,0:T(8,128)S(1)}, u32[]{:S(2)}, u32[]{:S(2)}) collective-permute-start(f32[8,128]{1,0:T(8,128)S(1)} %get-tuple-element.11), channel_id=1, source_target_pairs={{0,1},{1,2},{2,3},{3,4},{4,5},{5,6},{6,7},{7,0},{8,9},{9,10},{10,1... | collective-permute-start | bytes 12296 | tf_op jit(solution)/shard_map/ppermute | solution.py:71
  470.9 10.1 %collective-permute-start.22 = (f32[8,128]{1,0:T(8,128)S(1)}, f32[8,128]{1,0:T(8,128)S(1)}, u32[]{:S(2)}, u32[]{:S(2)}) collective-permute-start(f32[8,128]{1,0:T(8,128)S(1)} %get-tuple-element.11), channel_id=1, source_target_pairs={{0,7},{1,0},{2,1},{3,2},{4,3},{5,4},{6,5},{7,6},{8,15},{9,8},{10,9... | collective-permute-start | bytes 12296 | tf_op jit(solution)/shard_map/ppermute | solution.py:76
  481.0 6.3 %collective-permute-start.23 = (f32[8,128]{1,0:T(8,128)S(1)}, f32[8,128]{1,0:T(8,128)S(1)}, u32[]{:S(2)}, u32[]{:S(2)}) collective-permute-start(f32[8,128]{1,0:T(8,128)S(1)} %collective-permute-done.21), channel_id=1, source_target_pairs={{0,1},{1,2},{2,3},{3,4},{4,5},{5,6},{6,7},{7,0},{8,9},{9,10},{10,1... | collective-permute-start | bytes 12296 | tf_op jit(solution)/shard_map/ppermute | solution.py:71
  481.1 6.3 collective-permute-start.24
  487.3 6.3 %collective-permute-start.25 = (f32[8,128]{1,0:T(8,128)S(1)}, f32[8,128]{1,0:T(8,128)S(1)}, u32[]{:S(2)}, u32[]{:S(2)}) collective-permute-start(f32[8,128]{1,0:T(8,128)S(1)} %collective-permute-done.23), channel_id=1, source_target_pairs={{0,1},{1,2},{2,3},{3,4},{4,5},{5,6},{6,7},{7,0},{8,9},{9,10},{10,1... | collective-permute-start | bytes 12296 | tf_op jit(solution)/shard_map/ppermute | solution.py:71
  487.3 6.3 %collective-permute-start.26 = (f32[8,128]{1,0:T(8,128)S(1)}, f32[8,128]{1,0:T(8,128)S(1)}, u32[]{:S(2)}, u32[]{:S(2)}) collective-permute-start(f32[8,128]{1,0:T(8,128)S(1)} %collective-permute-done.24), channel_id=1, source_target_pairs={{0,7},{1,0},{2,1},{3,2},{4,3},{5,4},{6,5},{7,6},{8,15},{9,8},{10,9... | collective-permute-start | bytes 12296 | tf_op jit(solution)/shard_map/ppermute | solution.py:76
  493.6 6.3 %collective-permute-start.27 = (f32[8,128]{1,0:T(8,128)S(1)}, f32[8,128]{1,0:T(8,128)S(1)}, u32[]{:S(2)}, u32[]{:S(2)}) collective-permute-start(f32[8,128]{1,0:T(8,128)S(1)} %collective-permute-done.25), channel_id=1, source_target_pairs={{0,1},{1,2},{2,3},{3,4},{4,5},{5,6},{6,7},{7,0},{8,9},{9,10},{10,1... | collective-permute-start | bytes 12296 | tf_op jit(solution)/shard_map/ppermute | solution.py:71
  502.5 75.3 %reduce-scatter.21.cloned.1.call-start = ((), (), s32[]{:S(2)}) async-start(), calls=%async_computation.14 | async-start | bytes 36864 | tf_op jit(solution)/shard_map/reduce_scatter | solution.py:41
Sparse Core Ops, SparseCore 0:
  44.1 16.8 reduce-scatter.10
  64.1 54.7 reduce-scatter.8
  196.7 17.2 reduce-scatter.14
  217.0 54.7 reduce-scatter.12
  349.7 17.2 reduce-scatter.18
  369.9 54.7 reduce-scatter.16
  502.6 17.2 reduce-scatter.22
  523.0 54.7 reduce-scatter.20
